TPU v7x, 32 devices: a whole 2x2x4 slice. The times are simulated.
32 devices in a mesh: outer: 8 (over z, y), inner: 4 (over x, core).
Axes of the slice: x: 2, y: 2, z: 4, core: 2. Of those that a mesh axis runs over, the one named last changes fastest.
Arguments:
- x_in: bfloat16 [4096, 8192], P(('outer', 'inner')), may hold values from -6 to 6
- gate_in: bfloat16 [4096, 8192], P(('outer', 'inner')), may hold values from -6 to 6
- conv_weight: float32 [4, 8192], replicated, may hold values from -3 to 3
- conv_bias: float32 [8192], replicated, may hold values from -3 to 3
- x_proj: bfloat16 [8192, 288], replicated, may hold values from -0.0625 to 0.0625
- dt_proj: bfloat16 [256, 8192], replicated, may hold values from -0.375 to 0.375
- dt_bias: float32 [8192], replicated, may hold values from -9 to -2
- decay_rates: float32 [16, 8192], replicated, may hold values from 1 to 16
- skip_gain: float32 [8192], replicated, may hold values from 0.5 to 1.5
Outputs:
- gated_out: bfloat16 [4096, 8192], P(('outer', 'inner'))
All inputs are finite; a program needn't handle non-finite values.
Results may differ from a plain program's by a relative error of at most 0.0085.
Values may be sent and summed in bfloat16 or wider, within the bound.
No kernel may reach another device: no remote copies, remote signals or barrier semaphores. Data moves between devices by JAX's collectives and lax.ppermute only.
A program may use at most 192 MiB of HBM per device.

v0:
```python
import jax
import jax.numpy as jnp
from jax import lax
from jax.sharding import PartitionSpec as P

dt_ceiling = 0.25


def shifted(value, axis, steps):
    count = lax.axis_size(axis)
    initial, last = (max(0, -steps), min(count, count - steps))
    return lax.ppermute(value, axis, [(source, source + steps) for source in range(initial, last)])


def prefix(part, axis, combine, identity):
    place = lax.axis_index(axis)
    gathered = jax.tree.map(lambda a: lax.all_gather(a, axis), part)
    state = jax.tree.map(lambda a, e: jnp.zeros_like(a) + jnp.asarray(e, a.dtype), part, identity)

    def one(step, state):
        return combine(
            state, jax.tree.map(lambda a: lax.dynamic_index_in_dim(a, step, 0, False), gathered)
        )

    return lax.fori_loop(0, place, one, state)


def local(x_in, gate_in, conv_weight, conv_bias, x_proj, dt_proj, dt_bias, decay_rates, skip_gain):
    rows = x_in.shape[0]
    width = x_in.shape[1]
    taps = conv_weight.shape[0]
    rank = dt_proj.shape[0]
    states = decay_rates.shape[0]
    tail = x_in[rows - (taps - 1) :]
    prior = shifted(tail, ("outer", "inner"), 1)
    padded = jnp.concatenate([prior, x_in], axis=0).astype(jnp.float32)
    conv = conv_bias[None, :]
    for k in range(taps):
        conv = conv + conv_weight[k][None, :] * padded[k : k + rows]
    u_act = jax.nn.silu(conv).astype(jnp.bfloat16)
    proj = jnp.dot(u_act, x_proj, preferred_element_type=jnp.float32)
    dt_low = proj[:, :rank].astype(jnp.bfloat16)
    bmat = proj[:, rank : rank + states]
    cmat = proj[:, rank + states :]
    step_size = jnp.minimum(
        jax.nn.softplus(
            jnp.dot(dt_low, dt_proj, preferred_element_type=jnp.float32) + dt_bias[None, :]
        ),
        dt_ceiling,
    )
    ufloat = u_act.astype(jnp.float32)
    block = 16
    blocks = rows // block
    dt_blocks = step_size.reshape(blocks, block, width)
    in_blocks = (step_size * ufloat).reshape(blocks, block, width)
    b_blocks = bmat.reshape(blocks, block, states)
    c_blocks = cmat.reshape(blocks, block, states)

    def block_step(carry, inputs):
        state, offset = carry
        dt_blk, in_blk, b_blk, c_blk = inputs
        cumul = jnp.cumsum(dt_blk, axis=0)
        growth = cumul[:, None, :] * decay_rates[None, :, :]
        weighted = jnp.exp(growth) * b_blk[:, :, None] * in_blk[:, None, :]
        running = jnp.cumsum(weighted, axis=0)
        series = jnp.exp(-growth) * (state[None, :, :] + running)
        whole_cum = cumul + offset[None, :]
        return (
            (series[-1], whole_cum[-1]),
            (jnp.sum(c_blk[:, :, None] * series, axis=1), whole_cum),
        )

    start = (jnp.zeros((states, width), jnp.float32), jnp.zeros((width,), jnp.float32))
    finals, outs_pair = lax.scan(block_step, start, (dt_blocks, in_blocks, b_blocks, c_blocks))
    local_state, dt_total = finals
    local_out = outs_pair[0].reshape(rows, width)
    cum_blocks = outs_pair[1]
    neutral = (jnp.zeros((width,), jnp.float32), jnp.zeros((states, width), jnp.float32))

    def combine(earlier, later):
        return (
            earlier[0] + later[0],
            jnp.exp(-later[0][None, :] * decay_rates) * earlier[1] + later[1],
        )

    incoming = prefix((dt_total, local_state), ("outer", "inner"), combine, neutral)
    carry_state = incoming[1]

    def correction(inputs):
        c_blk, cum_blk = inputs
        faded = jnp.exp(-cum_blk[:, None, :] * decay_rates[None, :, :]) * carry_state[None, :, :]
        return jnp.sum(c_blk[:, :, None] * faded, axis=1)

    fixed = lax.map(correction, (c_blocks, cum_blocks)).reshape(rows, width)
    y_full = local_out + fixed + skip_gain[None, :] * ufloat
    return (y_full * jax.nn.silu(gate_in.astype(jnp.float32))).astype(jnp.bfloat16)


def solution(mesh):
    return jax.shard_map(
        local,
        mesh=mesh,
        in_specs=(
            P(("outer", "inner"), None),
            P(("outer", "inner"), None),
            P(),
            P(),
            P(),
            P(),
            P(),
            P(),
            P(),
        ),
        out_specs=P(("outer", "inner"), None),
        check_vma=False,
    )
```

profile of v0, /device:TPU:31, one launch (start us, length us, event | category | flops | bytes accessed | tf_op | source)
XLA Modules:
  0.0 371.2 jit_solution(10589194841650015512)
XLA Ops:
  10.8 2.3 maximum_convert_fusion
  13.2 2.7 multiply_convert_fusion
  16.0 1.4 fusion.23
  17.6 8.7 %convert_multiply_fusion.2 = (f32[128,8192]{1,0:T(8,128)}, f32[128,8192]{1,0:T(8,128)}) fusion(bf16[128,8192]{1,0:T(8,128)(2,1)S(1)} %multiply_convert_fusion, f32[8192]{0:T(1024)S(1)} %copy-done.7, bf16[256,8192]{1,0:T(8,128)(2,1)} %param.20, f32[128,288]{0,1:T(8,128)S(1)} %fusion.23), kind=kOutput, calls=%fused_computation.32 | convolution fusion | flops 547356672 | bytes 14778368 | tf_op jit(solution)/shard_map/dot_general | solution.py:47
  26.3 2.5 broadcast.46.clone
  28.8 2.4 broadcast.46.clone.1
  31.2 67.8 %while.38 = (s32[]{:T(128)}, f32[16,8192]{1,0:T(8,128)S(1)}, f32[8192]{0:T(1024)S(1)}, f32[8,16,8192]{2,1,0:T(8,128)}, f32[8,16,8192]{2,1,0:T(8,128)}, /*index=5...) while((s32[]{:T(128)}, f32[16,8192]{1,0:T(8,128)S(1)}, ...), condition=%wide.region_4.5_spmd, body=%wide.region_0.4_spmd.sunk | while | flops 52305920 | bytes 17504404 | solution.py:74
  33.9 4.6 %multiply_reduce_fusion.4 = (f32[16,8192]{1,0:T(8,128)S(1)}, f32[16,16,8192]{2,1,0:T(8,128)S(1)}) fusion(f32[16,16]{1,0:T(8,128)S(1)} %dynamic-slice_bitcast_fusion.10, f32[16,8192]{1,0:T(8,128)S(1)} %dynamic-slice_bitcast_fusion.11, f32[16,16]{1,0:T(8,128)S(1)} %dynamic-slice_bitcast_fusion.12, f32[16,8192]{1,0:T(8,128)S(1)} %get-tuple-element.427, ...), kind=kOutput, calls=%fused_computation.7.clone.1 | output fusion | flops 50200576 | bytes 11012096 | tf_op jit(solution)/shard_map/while/body/eval_jaxpr/jit(cumsum)/reduce_window_sum | solution.py:65
  42.4 4.6 %multiply_reduce_fusion.4 = (f32[16,8192]{1,0:T(8,128)S(1)}, f32[16,16,8192]{2,1,0:T(8,128)S(1)}) fusion(f32[16,16]{1,0:T(8,128)S(1)} %dynamic-slice_bitcast_fusion.10, f32[16,8192]{1,0:T(8,128)S(1)} %dynamic-slice_bitcast_fusion.11, f32[16,16]{1,0:T(8,128)S(1)} %dynamic-slice_bitcast_fusion.12, f32[16,8192]{1,0:T(8,128)S(1)} %get-tuple-element.427, ...), kind=kOutput, calls=%fused_computation.7.clone.1 | output fusion | flops 50200576 | bytes 11012096 | tf_op jit(solution)/shard_map/while/body/eval_jaxpr/jit(cumsum)/reduce_window_sum | solution.py:65
  50.9 4.6 %multiply_reduce_fusion.4 = (f32[16,8192]{1,0:T(8,128)S(1)}, f32[16,16,8192]{2,1,0:T(8,128)S(1)}) fusion(f32[16,16]{1,0:T(8,128)S(1)} %dynamic-slice_bitcast_fusion.10, f32[16,8192]{1,0:T(8,128)S(1)} %dynamic-slice_bitcast_fusion.11, f32[16,16]{1,0:T(8,128)S(1)} %dynamic-slice_bitcast_fusion.12, f32[16,8192]{1,0:T(8,128)S(1)} %get-tuple-element.427, ...), kind=kOutput, calls=%fused_computation.7.clone.1 | output fusion | flops 50200576 | bytes 11012096 | tf_op jit(solution)/shard_map/while/body/eval_jaxpr/jit(cumsum)/reduce_window_sum | solution.py:65
  59.4 4.6 %multiply_reduce_fusion.4 = (f32[16,8192]{1,0:T(8,128)S(1)}, f32[16,16,8192]{2,1,0:T(8,128)S(1)}) fusion(f32[16,16]{1,0:T(8,128)S(1)} %dynamic-slice_bitcast_fusion.10, f32[16,8192]{1,0:T(8,128)S(1)} %dynamic-slice_bitcast_fusion.11, f32[16,16]{1,0:T(8,128)S(1)} %dynamic-slice_bitcast_fusion.12, f32[16,8192]{1,0:T(8,128)S(1)} %get-tuple-element.427, ...), kind=kOutput, calls=%fused_computation.7.clone.1 | output fusion | flops 50200576 | bytes 11012096 | tf_op jit(solution)/shard_map/while/body/eval_jaxpr/jit(cumsum)/reduce_window_sum | solution.py:65
  67.9 4.6 %multiply_reduce_fusion.4 = (f32[16,8192]{1,0:T(8,128)S(1)}, f32[16,16,8192]{2,1,0:T(8,128)S(1)}) fusion(f32[16,16]{1,0:T(8,128)S(1)} %dynamic-slice_bitcast_fusion.10, f32[16,8192]{1,0:T(8,128)S(1)} %dynamic-slice_bitcast_fusion.11, f32[16,16]{1,0:T(8,128)S(1)} %dynamic-slice_bitcast_fusion.12, f32[16,8192]{1,0:T(8,128)S(1)} %get-tuple-element.427, ...), kind=kOutput, calls=%fused_computation.7.clone.1 | output fusion | flops 50200576 | bytes 11012096 | tf_op jit(solution)/shard_map/while/body/eval_jaxpr/jit(cumsum)/reduce_window_sum | solution.py:65
  76.3 4.6 %multiply_reduce_fusion.4 = (f32[16,8192]{1,0:T(8,128)S(1)}, f32[16,16,8192]{2,1,0:T(8,128)S(1)}) fusion(f32[16,16]{1,0:T(8,128)S(1)} %dynamic-slice_bitcast_fusion.10, f32[16,8192]{1,0:T(8,128)S(1)} %dynamic-slice_bitcast_fusion.11, f32[16,16]{1,0:T(8,128)S(1)} %dynamic-slice_bitcast_fusion.12, f32[16,8192]{1,0:T(8,128)S(1)} %get-tuple-element.427, ...), kind=kOutput, calls=%fused_computation.7.clone.1 | output fusion | flops 50200576 | bytes 11012096 | tf_op jit(solution)/shard_map/while/body/eval_jaxpr/jit(cumsum)/reduce_window_sum | solution.py:65
  84.8 4.6 %multiply_reduce_fusion.4 = (f32[16,8192]{1,0:T(8,128)S(1)}, f32[16,16,8192]{2,1,0:T(8,128)S(1)}) fusion(f32[16,16]{1,0:T(8,128)S(1)} %dynamic-slice_bitcast_fusion.10, f32[16,8192]{1,0:T(8,128)S(1)} %dynamic-slice_bitcast_fusion.11, f32[16,16]{1,0:T(8,128)S(1)} %dynamic-slice_bitcast_fusion.12, f32[16,8192]{1,0:T(8,128)S(1)} %get-tuple-element.427, ...), kind=kOutput, calls=%fused_computation.7.clone.1 | output fusion | flops 50200576 | bytes 11012096 | tf_op jit(solution)/shard_map/while/body/eval_jaxpr/jit(cumsum)/reduce_window_sum | solution.py:65
  93.3 4.6 %multiply_reduce_fusion.4 = (f32[16,8192]{1,0:T(8,128)S(1)}, f32[16,16,8192]{2,1,0:T(8,128)S(1)}) fusion(f32[16,16]{1,0:T(8,128)S(1)} %dynamic-slice_bitcast_fusion.10, f32[16,8192]{1,0:T(8,128)S(1)} %dynamic-slice_bitcast_fusion.11, f32[16,16]{1,0:T(8,128)S(1)} %dynamic-slice_bitcast_fusion.12, f32[16,8192]{1,0:T(8,128)S(1)} %get-tuple-element.427, ...), kind=kOutput, calls=%fused_computation.7.clone.1 | output fusion | flops 50200576 | bytes 11012096 | tf_op jit(solution)/shard_map/while/body/eval_jaxpr/jit(cumsum)/reduce_window_sum | solution.py:65
  100.4 54.6 %all-gather.5.cloned.1.call-done = f32[262144]{0:T(1024)} async-done(((f32[8192]{0:T(1024)}), f32[262144]{0:T(1024)}) %all-gather.5.cloned.1.call-update) | async-done | bytes 1048592 | tf_op jit(solution)/shard_map/all_gather | solution.py:17
  155.0 1.4 reshape.72
  156.4 114.1 %all-gather.7.cloned.1.call-done = f32[512,8192]{1,0:T(8,128)} async-done(((f32[16,8192]{1,0:T(8,128)}), f32[512,8192]{1,0:T(8,128)}) %all-gather.7.cloned.1.call-update) | async-done | bytes 16777232 | tf_op jit(solution)/shard_map/all_gather | solution.py:17
  270.6 44.1 %while.39 = (s32[]{:T(128)}, f32[16,8192]{1,0:T(8,128)S(1)}, s32[]{:T(128)}, f32[32,8192]{1,0:T(8,128)S(1)}, f32[16,8192]{1,0:T(8,128)S(1)}, /*index=5*/f32[32,16,8192]{2,1,0:T(8,128)}, s32[]{:T(128)}, s32[]{:T(128)}, s32[]{:T(128)}) while((s32[]{:T(128)}, f32[16,8192]{1,0:T(8,128)S(1)}, s32[]{:T(128)}, f32[32,8192]{1,0:T(8,128)S(1)}, ...), condition=%wide.region_6.7_spmd, body=%wide.region_5.6_spmd.sunk | while | flops 401413 | bytes 2195599 | solution.py:25
  272.1 1.4 bitcast_add_fusion.3
  314.7 2.4 broadcast.46
  317.1 36.7 %while.40 = (s32[]{:T(128)}, f32[8,16,8192]{2,1,0:T(8,128)}, f32[8,16,16]{2,1,0:T(8,128)S(1)}, f32[8,16,8192]{2,1,0:T(8,128)}, f32[16,8192]{1,0:T(8,128)S(1)}, /*index=5*/f32[16,8192]{1,0:T(8,128)S(1)}, s32[]{:T(128)}) while((s32[]{:T(128)}, f32[8,16,8192]{2,1,0:T(8,128)}, f32[8,16,16]{2,1,0:T(8,128)S(1)}, f32[8,16,8192]{2,1,0:T(8,128)}, ...), condition=%wide.region_9.10_spmd, body=%wide.region_7.9_spmd.sunk | while | flops 8388610 | bytes 4197473 | solution.py:94
  318.2 2.6 multiply_reduce_fusion.5
  322.8 2.6 multiply_reduce_fusion.5
  327.4 2.6 multiply_reduce_fusion.5
  332.0 2.6 multiply_reduce_fusion.5
  336.6 2.6 multiply_reduce_fusion.5
  341.2 2.6 multiply_reduce_fusion.5
  345.8 2.6 multiply_reduce_fusion.5
  350.4 2.6 multiply_reduce_fusion.5
  353.9 4.1 %add.107 = f32[8,16,8192]{2,1,0:T(8,128)S(1)} add(f32[8,16,8192]{2,1,0:T(8,128)} %get-tuple-element.143, f32[8,16,8192]{2,1,0:T(8,128)} %get-tuple-element.148) | non-fusion elementwise | flops 1048576 | bytes 12582912 | tf_op jit(solution)/shard_map/add | solution.py:95
  359.3 5.1 %fusion.12 = bf16[128,8192]{1,0:T(8,128)(2,1)} fusion(bf16[128,8192]{1,0:T(8,128)(2,1)S(1)} %copy-done.3, f32[8,16,8192]{2,1,0:T(8,128)S(1)} %add.107, f32[8192]{0:T(1024)S(1)} %copy-done.6, f32[131,8192]{1,0:T(8,128)S(1)} %bitcast.65, f32[8192]{0:T(1024)S(1)} %bitcast.79, f32[8192]{0:T(1024)S(1)} %bitcast.81, f32[8192]{0:T(1024)S(1)} %bitcast.77, ...), kind=kLoop, calls=%fused_computation.35 | loop fusion | flops 24117248 | bytes 25362432 | tf_op jit(solution)/shard_map/convert_element_type | solution.py:96
  (197 shorter events, 95.2 us)
Async XLA Ops:
  6.5 6.6 %copy-start.5 = (f32[8192]{0:T(1024)S(1)}, f32[8192]{0:T(1024)}, u32[]{:S(2)}) copy-start(f32[8192]{0:T(1024)} %param.18) | copy-start | bytes 98308
  6.5 148.5 %all-gather.5.cloned.1.call-start = ((), (), s32[]{:S(2)}) async-start(), calls=%async_computation | async-start | bytes 1081344 | tf_op jit(solution)/shard_map/all_gather | solution.py:17
  7.5 3.3 collective-permute-start
  10.8 5.1 %slice-start.2 = ((s8[4718592]{0:T(1024)(128)(4,1)}), s8[4194304]{0:T(1024)(128)(4,1)S(1)}, s32[]{:S(2)}) async-start(s8[4718592]{0:T(1024)(128)(4,1)} %bitcast.66), calls=%async_computation.4 | async-start | bytes 8388608
  13.2 2.8 copy-start
  13.2 2.8 slice-start.3
  16.0 1.7 copy-start.7
  26.3 4.9 %copy-start.1 = (f32[16,8192]{1,0:T(8,128)S(1)}, f32[16,8192]{1,0:T(8,128)}, u32[]{:S(2)}) copy-start(f32[16,8192]{1,0:T(8,128)} %param.22) | copy-start | bytes 1572868
  99.1 0.6 copy-start.4
  99.1 0.8 copy-start.2
  99.7 170.8 %all-gather.7.cloned.1.call-start = ((), (), s32[]{:S(2)}) async-start(), calls=%async_computation.1 | async-start | bytes 17301504 | tf_op jit(solution)/shard_map/all_gather | solution.py:17
  353.8 4.6 %slice-start = ((s8[4456448]{0:T(1024)(128)(4,1)}), s8[4194304]{0:T(1024)(128)(4,1)S(1)}, s32[]{:S(2)}) async-start(s8[4456448]{0:T(1024)(128)(4,1)} %bitcast.64), calls=%async_computation.2 | async-start | bytes 8388608
  353.9 4.7 %slice-start.1 = ((s8[4456448]{0:T(1024)(128)(4,1)}), s8[262144]{0:T(1024)(128)(4,1)S(1)}, s32[]{:S(2)}) async-start(s8[4456448]{0:T(1024)(128)(4,1)} %bitcast.64), calls=%async_computation.3 | async-start | bytes 524288
  353.9 5.4 %copy-start.3 = (bf16[128,8192]{1,0:T(8,128)(2,1)S(1)}, bf16[128,8192]{1,0:T(8,128)(2,1)}, u32[]{:S(2)}) copy-start(bf16[128,8192]{1,0:T(8,128)(2,1)} %param.16) | copy-start | bytes 6291460
  353.9 5.4 %copy-start.6 = (f32[8192]{0:T(1024)S(1)}, f32[8192]{0:T(1024)}, u32[]{:S(2)}) copy-start(f32[8192]{0:T(1024)} %param.23) | copy-start | bytes 98308
Sparse Core Ops, SparseCore 0:
  99.8 55.1 all-gather.4
  157.9 112.6 all-gather.6
where the time goes:
time: 374 us; the launch traced here: 371 us
  waiting for transfers between devices  170 us (45%)
  other arithmetic  137 us (37%)
  local copies, waits for them, and re-layouts  37.7 us (10%)
  between operations  13.6 us (4%)
  matrix products  10.1 us (3%)
    all_gather x2, waiting for transfers between devices, prefix(): gathered = jax.tree.map(lambda a: lax.all_gather(a, axis), part)  169 us
    add x31, other arithmetic, combine(): jnp.exp(-later[0][None, :] * decay_rates) * earlier[1] + later[1]  42.1 us
    another operation x8, other arithmetic, block_step(): running = jnp.cumsum(weighted, axis=0)  36.6 us
    reduce_sum x8, other arithmetic, correction(): return jnp.sum(c_blk[:, :, None] * faded, axis=1)  21.2 us
    dynamic_update_slice x8, other arithmetic, local(): lax.scan(block_step, start, (dt_blocks, in_blocks, b_blocks, c_blocks))  8.85 us
    mul x16, local copies, waits for them, and re-layouts, block_step(): weighted = jnp.exp(growth) * b_blk[:, :, None] * in_blk[:, None, :]  8.74 us
    squeeze x8, local copies, waits for them, and re-layouts, local(): lax.scan(block_step, start, (dt_blocks, in_blocks, b_blocks, c_blocks))  8.67 us
    dot_general x1, matrix products, local(): jnp.dot(dt_low, dt_proj, preferred_element_type=jnp.float32)  8.66 us
  transfers between devices with their start and end apart: 3, of which 3 were waited for; matrix products, arithmetic and copies ran while one was open for 1% of the time, Pallas kernels for 0%

commit v1 on v0

v1 whole, which is shorter than its diff:
```python
import jax
import jax.numpy as jnp
from jax import lax
from jax.experimental import pallas as pl
from jax.experimental.pallas import tpu as pltpu
from jax.sharding import PartitionSpec as P

AXES = ("outer", "inner")
LOG2E = 1.4426950408889634
DT_CEILING = 0.25
GROUP = 16
LANES = 128
F32 = jnp.float32
BF16 = jnp.bfloat16


def silu(value):
    half = 0.5 * value
    return half + half * jnp.tanh(half)


def capped_softplus(value):
    z = jnp.exp(jnp.minimum(value, -1.0))
    w = 1.0 + z
    return jnp.minimum(jnp.log(w) + (z - (w - 1.0)), DT_CEILING)


def pick_block(width, limit):
    block = limit
    while width % block:
        block //= 2
    return block


def spread_c(cmat, states, by_token):
    rows = cmat.shape[0]
    wide = GROUP * states
    n = lax.broadcasted_iota(jnp.int32, (states, wide), 0)
    col = lax.broadcasted_iota(jnp.int32, (states, wide), 1)
    pick = col % states if by_token else col // GROUP
    select = jnp.where(n == pick, 1.0, 0.0).astype(BF16)
    spread = jnp.dot(cmat.astype(BF16), select, preferred_element_type=F32)
    t = lax.broadcasted_iota(jnp.int32, (rows, wide), 0) % GROUP
    col = lax.broadcasted_iota(jnp.int32, (rows, wide), 1)
    token = col // states if by_token else col % GROUP
    return jnp.where(t == token, spread, 0.0).astype(BF16)


class Share:
    def __init__(self, width, parts, states):
        self.width = width // parts
        self.lanes = min(self.width, LANES)
        self.strips = self.width // self.lanes
        self.states = states
        self.rows = states * self.strips
        self.message_rows = -(-(self.rows + 2 * self.strips) // 8) * 8


def front(x_in, halo, conv_weight, conv_bias, x_proj_t, dt_proj, dt_bias, decay, skip, share):
    rows, width = x_in.shape
    taps = conv_weight.shape[0]
    rank = dt_proj.shape[0]
    states = decay.shape[0]
    columns = x_proj_t.shape[0]
    block = pick_block(width, 512)
    count = width // block
    per_block = block // share.width
    groups = rows // GROUP

    def body(x_hbm, halo_ref, cw_ref, cb_ref, xp_hbm, dp_hbm, bias_ref, a_ref, skip_ref,
             y_hbm, cum_hbm, msg_ref, bc_ref,
             x_s, xp_s, dp_s, u_s, y_s, cum_s, proj, low, hl, b_s, c_s, dt_s, v_s, h0_s, h1_s, add0_s, add1_s,
             x_sem, xp_sem, dp_sem, y_sem, cum_sem):
        h_s = (h0_s, h1_s)
        add_s = (add0_s, add1_s)

        def at(j):
            return pl.ds(pl.multiple_of(j * block, block), block)

        def copies_in(j):
            return (
                pltpu.make_async_copy(x_hbm.at[:, at(j)], x_s.at[:, at(j)], x_sem.at[j]),
                pltpu.make_async_copy(xp_hbm.at[:, at(j)], xp_s.at[:, at(j)], xp_sem.at[j]),
            )

        def copy_dp(j):
            return pltpu.make_async_copy(dp_hbm.at[:, at(j)], dp_s.at[:, at(j)], dp_sem.at[j])

        def copies_out(j):
            return (
                pltpu.make_async_copy(y_s.at[:, at(j)], y_hbm.at[:, at(j)], y_sem.at[j]),
                pltpu.make_async_copy(cum_s.at[:, at(j)], cum_hbm.at[:, at(j)], cum_sem.at[j]),
            )

        for j in range(count):
            for copy in copies_in(j):
                copy.start()
        for j in range(count):
            copy_dp(j).start()
        proj[...] = jnp.zeros_like(proj)

        top = lax.broadcasted_iota(jnp.int32, (8, block), 0)

        def head(j, _):
            for copy in copies_in(j):
                copy.wait()
            lanes = at(j)
            x = x_s[:, lanes].astype(F32)
            before = halo_ref[:, lanes]
            conv = cb_ref[:, lanes] + cw_ref[taps - 1 : taps, lanes] * x
            for k in range(1, taps):
                moved = pltpu.roll(x, k, 0)
                start = jnp.where(top < k, pltpu.roll(before, k, 0), moved[:8])
                moved = jnp.concatenate([start, moved[8:]], axis=0)
                conv = conv + cw_ref[taps - 1 - k : taps - k, lanes] * moved
            u = silu(conv).astype(BF16)
            u_s[:, lanes] = u
            proj[...] += lax.dot_general(u, xp_s[:, lanes], (((1,), (1,)), ((), ())), preferred_element_type=F32)
            return 0

        lax.fori_loop(0, count, head, 0)

        low[...] = proj[:, :rank].astype(BF16)
        bmat = proj[:, rank : rank + states]
        cmat = proj[:, rank + states : rank + 2 * states]
        bc_ref[...] = proj[:, rank:]
        c_s[...] = spread_c(cmat, states, True)
        high = bmat.astype(BF16).astype(F32)
        hl[...] = jnp.zeros_like(hl)
        hl[:, :states] = high
        hl[:, states : 2 * states] = bmat - high
        n = lax.broadcasted_iota(jnp.int32, (states, LANES), 0)
        lane = lax.broadcasted_iota(jnp.int32, (states, LANES), 1)
        keep = jnp.logical_or(lane == n, lane == n + states)
        ones = jnp.ones((LANES, LANES), BF16)
        token = lax.broadcasted_iota(jnp.int32, (GROUP * states, LANES), 1)
        own = lax.broadcasted_iota(jnp.int32, (GROUP * states, LANES), 0) // states

        def fill(g, _):
            base = pl.multiple_of(g * GROUP, GROUP)
            picked = [
                jnp.where(keep, jnp.broadcast_to(hl[pl.ds(base + i, 1), :], (states, LANES)), 0.0).astype(BF16)
                for i in range(GROUP)
            ]
            spread = jnp.dot(jnp.concatenate(picked, axis=0), ones, preferred_element_type=F32)
            b_s[g] = jnp.where(token == own, spread, 0.0)[:, :GROUP].astype(BF16)
            return 0

        lax.fori_loop(0, groups, fill, 0)

        row = lax.broadcasted_iota(jnp.int32, (rows, rows), 0)
        col = lax.broadcasted_iota(jnp.int32, (rows, rows), 1)
        tri = jnp.where(row >= col, 1.0, 0.0).astype(BF16)
        fill_rows = share.message_rows - share.rows - 2 * share.strips

        def tail(j, _):
            lanes = at(j)
            copy_dp(j).wait()
            raw = jnp.dot(low[...], dp_s[:, lanes], preferred_element_type=F32)
            dt = capped_softplus(raw + bias_ref[:, lanes])
            dt_s[...] = dt
            v_s[...] = (dt * u_s[:, lanes].astype(F32)).astype(BF16)
            cum = jnp.dot(tri, dt.astype(BF16), preferred_element_type=F32)
            cum_s[:, lanes] = cum.astype(BF16)
            total = cum[rows - 1 : rows]
            rates = a_ref[:, lanes] * (-LOG2E)
            skip_row = skip_ref[:, lanes]

            def load(g):
                add_s[g % 2][...] = jnp.dot(
                    b_s[g], v_s[g * GROUP : (g + 1) * GROUP, :], preferred_element_type=F32
                )

            def scan_group(g, h):
                for i in range(GROUP):
                    t = g * GROUP + i
                    at_i = slice(i * states, (i + 1) * states)
                    dtb = jnp.broadcast_to(dt_s[t : t + 1, :], (states, block))
                    h = jnp.exp2(dtb * rates) * h + add_s[g % 2][at_i, :]
                    h_s[g % 2][at_i, :] = h.astype(BF16)
                return h

            def emit(g):
                tokens = slice(g * GROUP, (g + 1) * GROUP)
                y = jnp.dot(c_s[tokens, :], h_s[g % 2][...], preferred_element_type=F32)
                y_s[tokens, lanes] = y + skip_row * u_s[tokens, lanes].astype(F32)

            h = jnp.zeros((states, block), F32)
            load(0)
            for g in range(groups):
                if g + 1 < groups:
                    load(g + 1)
                if g > 0:
                    emit(g - 1)
                h = scan_group(g, h)
            emit(groups - 1)
            for copy in copies_out(j):
                copy.start()
            high = total.astype(BF16).astype(F32)
            rest = total - high
            for p in range(per_block):
                cuts = [
                    slice(p * share.width + s * share.lanes, p * share.width + (s + 1) * share.lanes)
                    for s in range(share.strips)
                ]
                pieces = [h[:, c] for c in cuts] + [high[:, c] for c in cuts] + [rest[:, c] for c in cuts]
                if fill_rows:
                    pieces.append(jnp.zeros((fill_rows, share.lanes), F32))
                msg_ref[j * per_block + p] = jnp.concatenate(pieces, axis=0).astype(BF16)
            return 0

        lax.fori_loop(0, count, tail, 0)
        for j in range(count):
            for copy in copies_out(j):
                copy.wait()

    whole = pl.BlockSpec(memory_space=pltpu.VMEM)
    held = pl.BlockSpec(memory_space=pl.ANY)
    return pl.pallas_call(
        body,
        in_specs=[held, whole, whole, whole, held, held, whole, whole, whole],
        out_specs=[held, held, whole, whole],
        out_shape=[
            jax.ShapeDtypeStruct((rows, width), F32),
            jax.ShapeDtypeStruct((rows, width), BF16),
            jax.ShapeDtypeStruct((width // share.width, share.message_rows, share.lanes), BF16),
            jax.ShapeDtypeStruct((rows, 2 * states), F32),
        ],
        scratch_shapes=[
            pltpu.VMEM((rows, width), BF16),
            pltpu.VMEM((columns, width), BF16),
            pltpu.VMEM((rank, width), BF16),
            pltpu.VMEM((rows, width), BF16),
            pltpu.VMEM((rows, width), F32),
            pltpu.VMEM((rows, width), BF16),
            pltpu.VMEM((rows, columns), F32),
            pltpu.VMEM((rows, rank), BF16),
            pltpu.VMEM((rows, LANES), F32),
            pltpu.VMEM((groups, GROUP * states, GROUP), BF16),
            pltpu.VMEM((rows, GROUP * states), BF16),
            pltpu.VMEM((rows, block), F32),
            pltpu.VMEM((rows, block), BF16),
            pltpu.VMEM((GROUP * states, block), BF16),
            pltpu.VMEM((GROUP * states, block), BF16),
            pltpu.VMEM((GROUP * states, block), F32),
            pltpu.VMEM((GROUP * states, block), F32),
        ]
        + [pltpu.SemaphoreType.DMA((count,))] * 5,
        compiler_params=pltpu.CompilerParams(vmem_limit_bytes=40 * 2**20),
        name="front",
    )(x_in, halo, conv_weight, conv_bias, x_proj_t, dt_proj, dt_bias, decay, skip)


def combine(message, rates, share):
    parts = message.shape[0]
    states = share.states

    def body(msg_ref, a_ref, h_ref):
        rates = [a_ref[:, s * share.lanes : (s + 1) * share.lanes] * (-LOG2E) for s in range(share.strips)]

        def one(p, carry):
            later = []
            for s, h in enumerate(carry):
                h_ref[p, s * states : (s + 1) * states, :] = h.astype(BF16)
                high = msg_ref[p, share.rows + s : share.rows + s + 1, :].astype(F32)
                at = share.rows + share.strips + s
                total = high + msg_ref[p, at : at + 1, :].astype(F32)
                add = msg_ref[p, s * states : (s + 1) * states, :].astype(F32)
                later.append(jnp.exp2(rates[s] * total) * h + add)
            return tuple(later)

        zero = jnp.zeros((states, share.lanes), F32)
        lax.fori_loop(0, parts, one, (zero,) * share.strips, unroll=8)

    return pl.pallas_call(
        body, out_shape=jax.ShapeDtypeStruct((parts, share.rows, share.lanes), BF16), name="combine"
    )(message, rates)


def final(cum, h_in, y, gate, bc, decay, share):
    rows, width = cum.shape
    states = decay.shape[0]
    block = pick_block(width, 1024)
    sub = pick_block(block, 256)
    count = width // block
    per_block = block // share.width

    def body(cum_ref, h_ref, y_ref, gate_ref, bc_ref, a_ref, out_ref, c_s, a_s, hb_s):
        step = pl.program_id(0)

        @pl.when(step == 0)
        def _():
            c_s[...] = spread_c(bc_ref[:, states:], states, False)

        strips = [
            h_ref[p, s * states : (s + 1) * states, :].astype(F32)
            for p in range(per_block)
            for s in range(share.strips)
        ]
        h_in = jnp.concatenate(strips, axis=1)
        for n in range(states):
            a_s[n] = jnp.broadcast_to(a_ref[n : n + 1, :] * (-LOG2E), (GROUP, block)).astype(BF16)
            hb_s[n] = jnp.broadcast_to(h_in[n : n + 1, :], (GROUP, block)).astype(BF16)

        def strip(c, _):
            lanes = pl.ds(pl.multiple_of(c * sub, sub), sub)
            for g in range(rows // GROUP):
                at = slice(g * GROUP, (g + 1) * GROUP)
                cum = cum_ref[at, lanes]
                parts = [jnp.exp2(cum * a_s[n, :, lanes]) * hb_s[n, :, lanes] for n in range(states)]
                fixed = jnp.dot(c_s[at, :], jnp.concatenate(parts, axis=0), preferred_element_type=F32)
                gate = gate_ref[at, lanes].astype(F32)
                out_ref[at, lanes] = ((y_ref[at, lanes] + fixed) * silu(gate)).astype(BF16)
            return 0

        lax.fori_loop(0, block // sub, strip, 0)

    return pl.pallas_call(
        body,
        grid=(count,),
        in_specs=[
            pl.BlockSpec((rows, block), lambda i: (0, i)),
            pl.BlockSpec((per_block, share.rows, share.lanes), lambda i: (i, 0, 0)),
            pl.BlockSpec((rows, block), lambda i: (0, i)),
            pl.BlockSpec((rows, block), lambda i: (0, i)),
            pl.BlockSpec((rows, 2 * states), lambda i: (0, 0)),
            pl.BlockSpec((states, block), lambda i: (0, i)),
        ],
        out_specs=pl.BlockSpec((rows, block), lambda i: (0, i)),
        out_shape=jax.ShapeDtypeStruct((rows, width), BF16),
        scratch_shapes=[
            pltpu.VMEM((rows, GROUP * states), BF16),
            pltpu.VMEM((states, GROUP, block), BF16),
            pltpu.VMEM((states, GROUP, block), BF16),
        ],
        name="final",
    )(cum, h_in, y, gate, bc, decay)


def local(x_in, gate_in, conv_weight, conv_bias, x_proj, dt_proj, dt_bias, decay_rates, skip_gain):
    rows, width = x_in.shape
    taps = conv_weight.shape[0]
    states = decay_rates.shape[0]
    parts = lax.axis_size(AXES)
    share = Share(width, parts, states)
    prior = lax.ppermute(x_in[rows - (taps - 1) :], AXES, [(p, p + 1) for p in range(parts - 1)])
    halo = jnp.pad(prior.astype(F32), ((8 - (taps - 1), 0), (0, 0)))
    y, cum, message, bc = front(
        x_in, halo, conv_weight, conv_bias[None], x_proj.T, dt_proj, dt_bias[None], decay_rates, skip_gain[None], share
    )
    got = lax.all_to_all(message, AXES, 0, 0, tiled=True)
    own = lax.dynamic_slice_in_dim(decay_rates, lax.axis_index(AXES) * share.width, share.width, 1)
    incoming = combine(got, own, share)
    h_in = lax.all_to_all(incoming, AXES, 0, 0, tiled=True)
    return final(cum, h_in, y, gate_in, bc, decay_rates, share)


def solution(mesh):
    split = P(AXES, None)
    return jax.shard_map(
        local,
        mesh=mesh,
        in_specs=(split, split, P(), P(), P(), P(), P(), P(), P()),
        out_specs=split,
        check_vma=False,
    )
```

time: 374 us -> 103 us (0.28)
  the two profiles are of different devices: /device:TPU:31 before, /device:TPU:0 now
where the time goes in v1:
time: 103 us; the launch traced here: 102 us
  Pallas kernels  49.4 us (48%)
  local copies, waits for them, and re-layouts  14.9 us (14%)
  blocking collectives  13.9 us (13%)
  starting transfers between devices  12 us (12%)
  waiting for transfers between devices  11.6 us (11%)
    pallas_call x1, Pallas kernels, front(): pl.pallas_call(body, in_specs=[held, whole, whole, whole, held, held, who...  31.7 us
    pallas_call x1, Pallas kernels, final(): pl.pallas_call(body, grid=(count,), in_specs=[pl.BlockSpec((rows, block),...  15.8 us
    all_to_all x1, blocking collectives, local(): h_in = lax.all_to_all(incoming, AXES, 0, 0, tiled=True)  13.9 us
    unnamed x22, local copies, waits for them, and re-layouts  12.6 us
    all_to_all x1, waiting for transfers between devices, local(): got = lax.all_to_all(message, AXES, 0, 0, tiled=True)  10.7 us
    all_to_all x1, starting transfers between devices, local(): got = lax.all_to_all(message, AXES, 0, 0, tiled=True)  9.61 us
    ppermute x1, starting transfers between devices, local(): lax.ppermute(x_in[rows - (taps - 1):], AXES, [(p, p + 1) for p in range(p...  2.4 us
  transfers between devices with their start and end apart: 2, of which 2 were waited for; matrix products, arithmetic and copies ran while one was open for 1% of the time, Pallas kernels for 0%

profile of v1, /device:TPU:0, one launch (start us, length us, event | category | flops | bytes accessed | tf_op | source)
XLA Modules:
  0.0 101.8 jit_solution(9642832645322347567)
XLA Ops:
  0.0 0.9 slice.3
  0.9 2.4 %collective-permute-start = (bf16[3,8192]{1,0:T(4,128)(2,1)S(1)}, bf16[3,8192]{1,0:T(4,128)(2,1)S(1)}, u32[]{:S(2)}, u32[]{:S(2)}) collective-permute-start(bf16[3,8192]{1,0:T(4,128)(2,1)S(1)} %slice.3), channel_id=1, source_target_pairs={{0,1},{1,2},{2,3},{3,4},{4,5},{5,6},{6,7},{7,8},{8,9},{9,10},{10,1... | collective-permute-start | bytes 147464 | tf_op jit(solution)/shard_map/ppermute | solution.py:346
  3.4 0.9 collective-permute-done
  4.3 0.0 copy-start
  4.3 2.2 %copy-done = bf16[256,8192]{1,0:T(8,128)(2,1)S(1)} copy-done((bf16[256,8192]{1,0:T(8,128)(2,1)S(1)}, bf16[256,8192]{1,0:T(8,128)(2,1)}, u32[]{:S(2)}) %copy-start) | copy-done | bytes 4194328
  6.5 0.0 copy-start.2
  6.5 1.6 %copy-done.2 = bf16[128,8192]{1,0:T(8,128)(2,1)S(1)} copy-done((bf16[128,8192]{1,0:T(8,128)(2,1)S(1)}, bf16[128,8192]{1,0:T(8,128)(2,1)}, u32[]{:S(2)}) %copy-start.2) | copy-done | bytes 2097176
  8.1 0.0 copy-start.3
  8.1 1.0 %copy-done.3 = f32[16,8192]{1,0:T(8,128)S(1)} copy-done((f32[16,8192]{1,0:T(8,128)S(1)}, f32[16,8192]{1,0:T(8,128)}, u32[]{:S(2)}) %copy-start.3) | copy-done | bytes 524312
  9.1 0.0 copy-start.5
  9.1 0.9 copy-done.5
  10.0 0.0 copy-start.7
  10.0 0.8 copy-done.7
  10.8 0.0 copy-start.8
  10.8 0.8 copy-done.8
  11.5 0.0 copy-start.9
  11.5 0.8 copy-done.9
  12.3 31.7 %front.1 = (f32[128,8192]{1,0:T(8,128)S(1)}, bf16[128,8192]{1,0:T(8,128)(2,1)S(1)}, bf16[32,40,128]{2,1,0:T(8,128)(2,1)}, f32[128,32]{1,0:T(8,128)S(1)}) custom-call(bf16[128,8192]{1,0:T(8,128)(2,1)S(1)} %copy-done.2, f32[8,8192]{1,0:T(8,128)S(1)} %pad_convert_fusion.halo_ref, f32[4,8192]{1,0:T(4,128)S(1)} %copy-done.5, f32[1,8192]{1,0:T(1,128)S(1)} %bitcast.4, ...), custom_call_target="tpu_custom_call" | custom-call | tf_op jit(solution)/shard_map/front/pallas_call | solution.py:219
  44.0 0.0 copy-start.1
  44.0 1.9 %copy-done.1 = f32[128,8192]{1,0:T(8,128)} copy-done((f32[128,8192]{1,0:T(8,128)}, f32[128,8192]{1,0:T(8,128)S(1)}, u32[]{:S(2)}) %copy-start.1) | copy-done | bytes 4194328
  45.9 0.0 copy-start.4
  45.9 1.3 %copy-done.4 = bf16[128,8192]{1,0:T(8,128)(2,1)} copy-done((bf16[128,8192]{1,0:T(8,128)(2,1)}, bf16[128,8192]{1,0:T(8,128)(2,1)S(1)}, u32[]{:S(2)}) %copy-start.4) | copy-done | bytes 2097176
  47.3 0.0 copy-start.6
  47.3 0.6 copy-done.6
  47.9 9.6 %all-to-all-start = ((bf16[32,40,128]{2,1,0:T(8,128)(2,1)}), bf16[32,40,128]{2,1,0:T(8,128)(2,1)S(1)}, u32[]{:S(2)}, u32[]{:S(2)}) async-start(bf16[32,40,128]{2,1,0:T(8,128)(2,1)} %get-tuple-element.10), calls=%async_computation | async-start | bytes 655360 | tf_op jit(solution)/shard_map/all_to_all | solution.py:351
  57.5 1.3 %constant_dynamic-slice_fusion.a_ref = f32[16,256]{1,0:T(8,128)} fusion(f32[16,8192]{1,0:T(8,128)} %a_ref.3, s32[]{:T(128)S(6)} %select_n.3), kind=kLoop, calls=%fused_computation.1 | loop fusion | bytes 32772 | tf_op jit(solution)/shard_map/dynamic_slice | solution.py:352
  58.8 10.7 %all-to-all-done.msg_ref = bf16[32,40,128]{2,1,0:T(8,128)(2,1)S(1)} async-done(((bf16[32,40,128]{2,1,0:T(8,128)(2,1)}), bf16[32,40,128]{2,1,0:T(8,128)(2,1)S(1)}, u32[]{:S(2)}, u32[]{:S(2)}) %all-to-all-start) | async-done | bytes 327712 | tf_op jit(solution)/shard_map/all_to_all | solution.py:351
  69.6 0.0 copy-start.10
  69.6 0.7 copy-done.10
  70.3 1.8 %combine.1 = bf16[32,32,128]{2,1,0:T(8,128)(2,1)} custom-call(bf16[32,40,128]{2,1,0:T(8,128)(2,1)} %copy-done.10, f32[16,256]{1,0:T(8,128)} %constant_dynamic-slice_fusion.a_ref), custom_call_target="tpu_custom_call" | custom-call | tf_op jit(solution)/shard_map/combine/pallas_call | solution.py:275
  72.1 13.9 %all_to_all.10.h_ref = bf16[32,32,128]{2,1,0:T(8,128)(2,1)} all-to-all(bf16[32,32,128]{2,1,0:T(8,128)(2,1)} %combine.1), channel_id=1, replica_groups=mesh['outer'=8,'inner'=4] {'outer','inner'}, dimensions={0} | all-to-all | bytes 524288 | tf_op jit(solution)/shard_map/all_to_all | solution.py:354
  86.0 15.8 %final.1 = bf16[128,8192]{1,0:T(8,128)(2,1)} custom-call(bf16[128,8192]{1,0:T(8,128)(2,1)} %copy-done.4, bf16[32,32,128]{2,1,0:T(8,128)(2,1)} %all_to_all.10.h_ref, f32[128,8192]{1,0:T(8,128)} %copy-done.1, bf16[128,8192]{1,0:T(8,128)(2,1)} %gate_ref.1, f32[128,32]{1,0:T(8,128)} %copy-done.6, f32[16,8192]{1,0:T(8,128)} %a_ref.3), custom_call_target="tpu_custom_call" | custom-call | tf_op jit(solution)/shard_map/final/pallas_call | solution.py:318
  (1 shorter events, 0.0 us)
Async XLA Ops:
  0.9 3.3 %collective-permute-start = (bf16[3,8192]{1,0:T(4,128)(2,1)S(1)}, bf16[3,8192]{1,0:T(4,128)(2,1)S(1)}, u32[]{:S(2)}, u32[]{:S(2)}) collective-permute-start(bf16[3,8192]{1,0:T(4,128)(2,1)S(1)} %slice.3), channel_id=1, source_target_pairs={{0,1},{1,2},{2,3},{3,4},{4,5},{5,6},{6,7},{7,8},{8,9},{9,10},{10,1... | collective-permute-start | bytes 147464 | tf_op jit(solution)/shard_map/ppermute | solution.py:346
  4.3 2.2 %copy-start = (bf16[256,8192]{1,0:T(8,128)(2,1)S(1)}, bf16[256,8192]{1,0:T(8,128)(2,1)}, u32[]{:S(2)}) copy-start(bf16[256,8192]{1,0:T(8,128)(2,1)} %dp_hbm.1) | copy-start | bytes 12582916
  6.5 1.6 %copy-start.2 = (bf16[128,8192]{1,0:T(8,128)(2,1)S(1)}, bf16[128,8192]{1,0:T(8,128)(2,1)}, u32[]{:S(2)}) copy-start(bf16[128,8192]{1,0:T(8,128)(2,1)} %x_hbm.1) | copy-start | bytes 6291460
  8.1 1.0 %copy-start.3 = (f32[16,8192]{1,0:T(8,128)S(1)}, f32[16,8192]{1,0:T(8,128)}, u32[]{:S(2)}) copy-start(f32[16,8192]{1,0:T(8,128)} %a_ref.3) | copy-start | bytes 1572868
  9.1 0.9 copy-start.5
  10.0 0.8 copy-start.7
  10.8 0.8 copy-start.8
  11.5 0.8 copy-start.9
  44.0 1.9 %copy-start.1 = (f32[128,8192]{1,0:T(8,128)}, f32[128,8192]{1,0:T(8,128)S(1)}, u32[]{:S(2)}) copy-start(f32[128,8192]{1,0:T(8,128)S(1)} %get-tuple-element.11.y_ref) | copy-start | bytes 12582916
  45.9 1.3 %copy-start.4 = (bf16[128,8192]{1,0:T(8,128)(2,1)}, bf16[128,8192]{1,0:T(8,128)(2,1)S(1)}, u32[]{:S(2)}) copy-start(bf16[128,8192]{1,0:T(8,128)(2,1)S(1)} %get-tuple-element.9.cum_ref) | copy-start | bytes 6291460
  47.3 0.6 copy-start.6
  47.9 21.7 %all-to-all-start = ((bf16[32,40,128]{2,1,0:T(8,128)(2,1)}), bf16[32,40,128]{2,1,0:T(8,128)(2,1)S(1)}, u32[]{:S(2)}, u32[]{:S(2)}) async-start(bf16[32,40,128]{2,1,0:T(8,128)(2,1)} %get-tuple-element.10), calls=%async_computation | async-start | bytes 655360 | tf_op jit(solution)/shard_map/all_to_all | solution.py:351
  69.6 0.7 copy-start.10

commit v2 on v1

--- a/solution.py
+++ b/solution.py
@@ -10,6 +10,9 @@
 DT_CEILING = 0.25
 GROUP = 16
 LANES = 128
+HALO = 16
+AHEAD = 2
+VMEM_BYTES = 60 * 2**20
 F32 = jnp.float32
 BF16 = jnp.bfloat16
 
@@ -62,63 +65,105 @@
     rank = dt_proj.shape[0]
     states = decay.shape[0]
     columns = x_proj_t.shape[0]
-    block = pick_block(width, 512)
+    block = pick_block(width, 1024)
     count = width // block
     per_block = block // share.width
     groups = rows // GROUP
-
-    def body(x_hbm, halo_ref, cw_ref, cb_ref, xp_hbm, dp_hbm, bias_ref, a_ref, skip_ref,
+    wide = pick_block(width, 1024)
+    chunks = width // wide
+    ratio = wide // block
+
+    def body(x_hbm, halo_hbm, cw_hbm, cb_hbm, xp_hbm, dp_hbm, bias_hbm, a_hbm, skip_hbm,
              y_hbm, cum_hbm, msg_ref, bc_ref,
-             x_s, xp_s, dp_s, u_s, y_s, cum_s, proj, low, hl, b_s, c_s, dt_s, v_s, h0_s, h1_s, add0_s, add1_s,
-             x_sem, xp_sem, dp_sem, y_sem, cum_sem):
+             x_s, xp_s, dp_s, u_s, y_s, cum_s, cw_ref, cb_ref, bias_ref, a_ref, skip_ref,
+             halo_s, proj, low, hl, b_s, c_s, dt_s, v_s, h0_s, h1_s, add0_s, add1_s, rates, shift_s,
+             x_sem, xp_sem, dp_sem, y_sem, cum_sem, small_sem):
         h_s = (h0_s, h1_s)
         add_s = (add0_s, add1_s)
+        small = [
+            pltpu.make_async_copy(source, target, small_sem.at[i])
+            for i, (source, target) in enumerate(
+                (
+                    (halo_hbm, halo_s),
+                    (cw_hbm, cw_ref),
+                    (cb_hbm, cb_ref),
+                    (a_hbm, a_ref),
+                    (bias_hbm, bias_ref),
+                    (skip_hbm, skip_ref),
+                )
+            )
+        ]
 
         def at(j):
             return pl.ds(pl.multiple_of(j * block, block), block)
 
-        def copies_in(j):
+        def chunk(c):
+            return pl.ds(pl.multiple_of(c * wide, wide), wide)
+
+        def copies_in(c):
             return (
-                pltpu.make_async_copy(x_hbm.at[:, at(j)], x_s.at[:, at(j)], x_sem.at[j]),
-                pltpu.make_async_copy(xp_hbm.at[:, at(j)], xp_s.at[:, at(j)], xp_sem.at[j]),
+                pltpu.make_async_copy(x_hbm.at[:, chunk(c)], x_s.at[:rows, chunk(c)], x_sem.at[c]),
+                pltpu.make_async_copy(xp_hbm.at[:, chunk(c)], xp_s.at[:, chunk(c)], xp_sem.at[c]),
             )
 
-        def copy_dp(j):
-            return pltpu.make_async_copy(dp_hbm.at[:, at(j)], dp_s.at[:, at(j)], dp_sem.at[j])
-
-        def copies_out(j):
+        def copy_dp(c):
+            return pltpu.make_async_copy(dp_hbm.at[:, chunk(c)], dp_s.at[:, chunk(c)], dp_sem.at[c])
+
+        def copies_out(c):
             return (
-                pltpu.make_async_copy(y_s.at[:, at(j)], y_hbm.at[:, at(j)], y_sem.at[j]),
-                pltpu.make_async_copy(cum_s.at[:, at(j)], cum_hbm.at[:, at(j)], cum_sem.at[j]),
+                pltpu.make_async_copy(y_s.at[:, chunk(c)], y_hbm.at[:, chunk(c)], y_sem.at[c]),
+                pltpu.make_async_copy(cum_s.at[:, chunk(c)], cum_hbm.at[:, chunk(c)], cum_sem.at[c]),
             )
 
-        for j in range(count):
-            for copy in copies_in(j):
+        for copy in small[:3]:
+            copy.start()
+        for c in range(min(AHEAD, chunks)):
+            for copy in copies_in(c):
                 copy.start()
-        for j in range(count):
-            copy_dp(j).start()
         proj[...] = jnp.zeros_like(proj)
 
-        top = lax.broadcasted_iota(jnp.int32, (8, block), 0)
-
-        def head(j, _):
-            for copy in copies_in(j):
-                copy.wait()
+        line = lax.broadcasted_iota(jnp.int32, (rows, rows + HALO), 0)
+        source = lax.broadcasted_iota(jnp.int32, (rows, rows + HALO), 1)
+        for k in range(taps):
+            want = line - (taps - 1 - k)
+            want = jnp.where(want < 0, want + rows + taps - 1, want)
+            shift_s[k * rows : (k + 1) * rows, :] = jnp.where(source == want, 1.0, 0.0).astype(BF16)
+        x_s[rows:, :] = jnp.zeros((HALO, width), BF16)
+        for copy in small[:3]:
+            copy.wait()
+        x_s[rows : rows + taps - 1, :] = halo_s[...]
+
+        def head(j):
             lanes = at(j)
-            x = x_s[:, lanes].astype(F32)
-            before = halo_ref[:, lanes]
-            conv = cb_ref[:, lanes] + cw_ref[taps - 1 : taps, lanes] * x
-            for k in range(1, taps):
-                moved = pltpu.roll(x, k, 0)
-                start = jnp.where(top < k, pltpu.roll(before, k, 0), moved[:8])
-                moved = jnp.concatenate([start, moved[8:]], axis=0)
-                conv = conv + cw_ref[taps - 1 - k : taps - k, lanes] * moved
+            moved = jnp.dot(shift_s[...], x_s[:, lanes], preferred_element_type=F32)
+            conv = cb_ref[:, lanes]
+            for k in range(taps):
+                conv = conv + cw_ref[k : k + 1, lanes] * moved[k * rows : (k + 1) * rows]
             u = silu(conv).astype(BF16)
             u_s[:, lanes] = u
             proj[...] += lax.dot_general(u, xp_s[:, lanes], (((1,), (1,)), ((), ())), preferred_element_type=F32)
+
+        def head_chunk(c, _):
+            for copy in copies_in(c):
+                copy.wait()
+
+            @pl.when(c + AHEAD < chunks)
+            def _():
+                for copy in copies_in(c + AHEAD):
+                    copy.start()
+
+            @pl.when(c + AHEAD == chunks)
+            def _():
+                for copy in small[3:]:
+                    copy.start()
+                for d in range(chunks):
+                    copy_dp(d).start()
+
+            for r in range(ratio):
+                head(c * ratio + r)
             return 0
 
-        lax.fori_loop(0, count, head, 0)
+        lax.fori_loop(0, chunks, head_chunk, 0)
 
         low[...] = proj[:, :rank].astype(BF16)
         bmat = proj[:, rank : rank + states]
@@ -151,11 +196,17 @@
         row = lax.broadcasted_iota(jnp.int32, (rows, rows), 0)
         col = lax.broadcasted_iota(jnp.int32, (rows, rows), 1)
         tri = jnp.where(row >= col, 1.0, 0.0).astype(BF16)
+        for copy in small[3:]:
+            copy.wait()
         fill_rows = share.message_rows - share.rows - 2 * share.strips
 
         def tail(j, _):
             lanes = at(j)
-            copy_dp(j).wait()
+
+            @pl.when(j % ratio == 0)
+            def _():
+                copy_dp(j // ratio).wait()
+
             raw = jnp.dot(low[...], dp_s[:, lanes], preferred_element_type=F32)
             dt = capped_softplus(raw + bias_ref[:, lanes])
             dt_s[...] = dt
@@ -163,7 +214,7 @@
             cum = jnp.dot(tri, dt.astype(BF16), preferred_element_type=F32)
             cum_s[:, lanes] = cum.astype(BF16)
             total = cum[rows - 1 : rows]
-            rates = a_ref[:, lanes] * (-LOG2E)
+            rates[...] = a_ref[:, lanes] * (-LOG2E)
             skip_row = skip_ref[:, lanes]
 
             def load(g):
@@ -176,7 +227,7 @@
                     t = g * GROUP + i
                     at_i = slice(i * states, (i + 1) * states)
                     dtb = jnp.broadcast_to(dt_s[t : t + 1, :], (states, block))
-                    h = jnp.exp2(dtb * rates) * h + add_s[g % 2][at_i, :]
+                    h = jnp.exp2(dtb * rates[...]) * h + add_s[g % 2][at_i, :]
                     h_s[g % 2][at_i, :] = h.astype(BF16)
                 return h
 
@@ -194,8 +245,12 @@
                     emit(g - 1)
                 h = scan_group(g, h)
             emit(groups - 1)
-            for copy in copies_out(j):
-                copy.start()
+
+            @pl.when(j % ratio == ratio - 1)
+            def _():
+                for copy in copies_out(j // ratio):
+                    copy.start()
+
             high = total.astype(BF16).astype(F32)
             rest = total - high
             for p in range(per_block):
@@ -210,15 +265,15 @@
             return 0
 
         lax.fori_loop(0, count, tail, 0)
-        for j in range(count):
-            for copy in copies_out(j):
+        for c in range(chunks):
+            for copy in copies_out(c):
                 copy.wait()
 
     whole = pl.BlockSpec(memory_space=pltpu.VMEM)
-    held = pl.BlockSpec(memory_space=pl.ANY)
+    held = pl.BlockSpec(memory_space=pltpu.HBM)
     return pl.pallas_call(
         body,
-        in_specs=[held, whole, whole, whole, held, held, whole, whole, whole],
+        in_specs=[held] * 9,
         out_specs=[held, held, whole, whole],
         out_shape=[
             jax.ShapeDtypeStruct((rows, width), F32),
@@ -227,12 +282,18 @@
             jax.ShapeDtypeStruct((rows, 2 * states), F32),
         ],
         scratch_shapes=[
-            pltpu.VMEM((rows, width), BF16),
+            pltpu.VMEM((rows + HALO, width), BF16),
             pltpu.VMEM((columns, width), BF16),
             pltpu.VMEM((rank, width), BF16),
             pltpu.VMEM((rows, width), BF16),
             pltpu.VMEM((rows, width), F32),
             pltpu.VMEM((rows, width), BF16),
+            pltpu.VMEM((taps, width), F32),
+            pltpu.VMEM((1, width), F32),
+            pltpu.VMEM((1, width), F32),
+            pltpu.VMEM((states, width), F32),
+            pltpu.VMEM((1, width), F32),
+            pltpu.VMEM((taps - 1, width), BF16),
             pltpu.VMEM((rows, columns), F32),
             pltpu.VMEM((rows, rank), BF16),
             pltpu.VMEM((rows, LANES), F32),
@@ -244,19 +305,31 @@
             pltpu.VMEM((GROUP * states, block), BF16),
             pltpu.VMEM((GROUP * states, block), F32),
             pltpu.VMEM((GROUP * states, block), F32),
+            pltpu.VMEM((states, block), F32),
+            pltpu.VMEM((taps * rows, rows + HALO), BF16),
         ]
-        + [pltpu.SemaphoreType.DMA((count,))] * 5,
-        compiler_params=pltpu.CompilerParams(vmem_limit_bytes=40 * 2**20),
+        + [pltpu.SemaphoreType.DMA((chunks,))] * 5
+        + [pltpu.SemaphoreType.DMA((6,))],
+        compiler_params=pltpu.CompilerParams(vmem_limit_bytes=VMEM_BYTES),
         name="front",
     )(x_in, halo, conv_weight, conv_bias, x_proj_t, dt_proj, dt_bias, decay, skip)
 
 
-def combine(message, rates, share):
+def combine(message, decay, mine, share):
     parts = message.shape[0]
     states = share.states
-
-    def body(msg_ref, a_ref, h_ref):
-        rates = [a_ref[:, s * share.lanes : (s + 1) * share.lanes] * (-LOG2E) for s in range(share.strips)]
+    aligned = share.width % LANES == 0
+    if not aligned:
+        decay = lax.dynamic_slice_in_dim(decay, mine * share.width, share.width, 1)
+
+    def body(mine_ref, msg_ref, a_hbm, h_ref, a_s, sem):
+        source = a_hbm
+        if aligned:
+            source = a_hbm.at[:, pl.ds(pl.multiple_of(mine_ref[0] * share.width, LANES), share.width)]
+        copy = pltpu.make_async_copy(source, a_s, sem.at[0])
+        copy.start()
+        copy.wait()
+        rates = [a_s[:, s * share.lanes : (s + 1) * share.lanes] * (-LOG2E) for s in range(share.strips)]
 
         def one(p, carry):
             later = []
@@ -272,67 +345,108 @@
         zero = jnp.zeros((states, share.lanes), F32)
         lax.fori_loop(0, parts, one, (zero,) * share.strips, unroll=8)
 
+    whole = pl.BlockSpec(memory_space=pltpu.VMEM)
     return pl.pallas_call(
-        body, out_shape=jax.ShapeDtypeStruct((parts, share.rows, share.lanes), BF16), name="combine"
-    )(message, rates)
+        body,
+        in_specs=[pl.BlockSpec(memory_space=pltpu.SMEM), whole, pl.BlockSpec(memory_space=pltpu.HBM)],
+        out_specs=whole,
+        out_shape=jax.ShapeDtypeStruct((parts, share.rows, share.lanes), BF16),
+        scratch_shapes=[pltpu.VMEM((states, share.width), F32), pltpu.SemaphoreType.DMA((1,))],
+        name="combine",
+    )(mine[None], message, decay)
 
 
 def final(cum, h_in, y, gate, bc, decay, share):
     rows, width = cum.shape
     states = decay.shape[0]
-    block = pick_block(width, 1024)
-    sub = pick_block(block, 256)
+    wide = pick_block(width, 1024)
+    block = pick_block(wide, 256)
     count = width // block
+    chunks = width // wide
+    ratio = wide // block
     per_block = block // share.width
 
-    def body(cum_ref, h_ref, y_ref, gate_ref, bc_ref, a_ref, out_ref, c_s, a_s, hb_s):
-        step = pl.program_id(0)
-
-        @pl.when(step == 0)
-        def _():
-            c_s[...] = spread_c(bc_ref[:, states:], states, False)
-
-        strips = [
-            h_ref[p, s * states : (s + 1) * states, :].astype(F32)
-            for p in range(per_block)
-            for s in range(share.strips)
-        ]
-        h_in = jnp.concatenate(strips, axis=1)
-        for n in range(states):
-            a_s[n] = jnp.broadcast_to(a_ref[n : n + 1, :] * (-LOG2E), (GROUP, block)).astype(BF16)
-            hb_s[n] = jnp.broadcast_to(h_in[n : n + 1, :], (GROUP, block)).astype(BF16)
-
-        def strip(c, _):
-            lanes = pl.ds(pl.multiple_of(c * sub, sub), sub)
+    def body(cum_hbm, h_ref, y_hbm, gate_hbm, bc_ref, a_hbm, out_hbm,
+             cum_s, y_s, gate_s, out_s, a_ref, c_s, cum_sem, y_sem, gate_sem, out_sem, a_sem):
+        def at(j):
+            return pl.ds(pl.multiple_of(j * block, block), block)
+
+        def chunk(c):
+            return pl.ds(pl.multiple_of(c * wide, wide), wide)
+
+        def copies_in(c):
+            return (
+                pltpu.make_async_copy(cum_hbm.at[:, chunk(c)], cum_s.at[:, chunk(c)], cum_sem.at[c]),
+                pltpu.make_async_copy(y_hbm.at[:, chunk(c)], y_s.at[:, chunk(c)], y_sem.at[c]),
+                pltpu.make_async_copy(gate_hbm.at[:, chunk(c)], gate_s.at[:, chunk(c)], gate_sem.at[c]),
+            )
+
+        def copy_out(c):
+            return pltpu.make_async_copy(out_s.at[:, chunk(c)], out_hbm.at[:, chunk(c)], out_sem.at[c])
+
+        copy_a = pltpu.make_async_copy(a_hbm, a_ref, a_sem.at[0])
+        copy_a.start()
+        for c in range(min(AHEAD, chunks)):
+            for copy in copies_in(c):
+                copy.start()
+        c_s[...] = spread_c(bc_ref[:, states:], states, False)
+        copy_a.wait()
+
+        def strip(j, _):
+            lanes = at(j)
+            strips = [
+                h_ref[j * per_block + p, s * states : (s + 1) * states, :].astype(F32)
+                for p in range(per_block)
+                for s in range(share.strips)
+            ]
+            h_in = jnp.concatenate(strips, axis=1)
+            rates = a_ref[:, lanes] * (-LOG2E)
+            a_n = [jnp.broadcast_to(rates[n : n + 1], (GROUP, block)).astype(BF16) for n in range(states)]
+            h_n = [jnp.broadcast_to(h_in[n : n + 1], (GROUP, block)).astype(BF16) for n in range(states)]
             for g in range(rows // GROUP):
-                at = slice(g * GROUP, (g + 1) * GROUP)
-                cum = cum_ref[at, lanes]
-                parts = [jnp.exp2(cum * a_s[n, :, lanes]) * hb_s[n, :, lanes] for n in range(states)]
-                fixed = jnp.dot(c_s[at, :], jnp.concatenate(parts, axis=0), preferred_element_type=F32)
-                gate = gate_ref[at, lanes].astype(F32)
-                out_ref[at, lanes] = ((y_ref[at, lanes] + fixed) * silu(gate)).astype(BF16)
+                tokens = slice(g * GROUP, (g + 1) * GROUP)
+                cum = cum_s[tokens, lanes]
+                parts = [jnp.exp2(cum * a_n[n]) * h_n[n] for n in range(states)]
+                fixed = jnp.dot(c_s[tokens, :], jnp.concatenate(parts, axis=0), preferred_element_type=F32)
+                gate = gate_s[tokens, lanes].astype(F32)
+                out_s[tokens, lanes] = ((y_s[tokens, lanes] + fixed) * silu(gate)).astype(BF16)
             return 0
 
-        lax.fori_loop(0, block // sub, strip, 0)
-
+        def run_chunk(c, _):
+            for copy in copies_in(c):
+                copy.wait()
+
+            @pl.when(c + AHEAD < chunks)
+            def _():
+                for copy in copies_in(c + AHEAD):
+                    copy.start()
+
+            lax.fori_loop(c * ratio, (c + 1) * ratio, strip, 0)
+            copy_out(c).start()
+            return 0
+
+        lax.fori_loop(0, chunks, run_chunk, 0)
+        for c in range(chunks):
+            copy_out(c).wait()
+
+    whole = pl.BlockSpec(memory_space=pltpu.VMEM)
+    held = pl.BlockSpec(memory_space=pltpu.HBM)
     return pl.pallas_call(
         body,
-        grid=(count,),
-        in_specs=[
-            pl.BlockSpec((rows, block), lambda i: (0, i)),
-            pl.BlockSpec((per_block, share.rows, share.lanes), lambda i: (i, 0, 0)),
-            pl.BlockSpec((rows, block), lambda i: (0, i)),
-            pl.BlockSpec((rows, block), lambda i: (0, i)),
-            pl.BlockSpec((rows, 2 * states), lambda i: (0, 0)),
-            pl.BlockSpec((states, block), lambda i: (0, i)),
-        ],
-        out_specs=pl.BlockSpec((rows, block), lambda i: (0, i)),
+        in_specs=[held, whole, held, held, whole, held],
+        out_specs=held,
         out_shape=jax.ShapeDtypeStruct((rows, width), BF16),
         scratch_shapes=[
+            pltpu.VMEM((rows, width), BF16),
+            pltpu.VMEM((rows, width), F32),
+            pltpu.VMEM((rows, width), BF16),
+            pltpu.VMEM((rows, width), BF16),
+            pltpu.VMEM((states, width), F32),
             pltpu.VMEM((rows, GROUP * states), BF16),
-            pltpu.VMEM((states, GROUP, block), BF16),
-            pltpu.VMEM((states, GROUP, block), BF16),
-        ],
+        ]
+        + [pltpu.SemaphoreType.DMA((chunks,))] * 4
+        + [pltpu.SemaphoreType.DMA((1,))],
+        compiler_params=pltpu.CompilerParams(vmem_limit_bytes=VMEM_BYTES),
         name="final",
     )(cum, h_in, y, gate, bc, decay)
 
@@ -344,13 +458,12 @@
     parts = lax.axis_size(AXES)
     share = Share(width, parts, states)
     prior = lax.ppermute(x_in[rows - (taps - 1) :], AXES, [(p, p + 1) for p in range(parts - 1)])
-    halo = jnp.pad(prior.astype(F32), ((8 - (taps - 1), 0), (0, 0)))
+    mine = lax.axis_index(AXES).astype(jnp.int32)
     y, cum, message, bc = front(
-        x_in, halo, conv_weight, conv_bias[None], x_proj.T, dt_proj, dt_bias[None], decay_rates, skip_gain[None], share
+        x_in, prior, conv_weight, conv_bias[None], x_proj.T, dt_proj, dt_bias[None], decay_rates, skip_gain[None], share
     )
     got = lax.all_to_all(message, AXES, 0, 0, tiled=True)
-    own = lax.dynamic_slice_in_dim(decay_rates, lax.axis_index(AXES) * share.width, share.width, 1)
-    incoming = combine(got, own, share)
+    incoming = combine(got, decay_rates, mine, share)
     h_in = lax.all_to_all(incoming, AXES, 0, 0, tiled=True)
     return final(cum, h_in, y, gate_in, bc, decay_rates, share)
 

time: 103 us -> 90.7 us (0.88)
  local copies, waits for them, and re-layouts: 14.9 us -> 2.29 us
  waiting for transfers between devices: 11.6 us -> 12.9 us
    unnamed x22 -> x4, local copies, waits for them, and re-layouts: 12.6 us -> 1.35 us
    all_to_all x1, waiting for transfers between devices: 10.7 us -> 12 us  [local(): got = lax.all_to_all(message, AXES, 0, 0, tiled=True)]
    dynamic_slice x1 -> x0, local copies, waits for them, and re-layouts: 1.32 us -> none  [local(): lax.dynamic_slice_in_dim(decay_rates, lax.axis_index(AXES) * share.width,...]
  transfers between devices with their start and end apart: 2 -> 2, of which waited for: 2 -> 2; matrix products, arithmetic and copies ran while one was open for 1% -> 0% of each run, Pallas kernels for 0% -> 0%
where the time goes in v2:
time: 90.7 us; the launch traced here: 90.3 us
  Pallas kernels  49.1 us (54%)
  blocking collectives  13.9 us (15%)
  waiting for transfers between devices  12.9 us (14%)
  starting transfers between devices  12 us (13%)
  local copies, waits for them, and re-layouts  2.29 us (3%)
    pallas_call x1, Pallas kernels, front(): pl.pallas_call(body, in_specs=[held] * 9, out_specs=[held, held, whole, w...  30.3 us
    pallas_call x1, Pallas kernels, final(): pl.pallas_call(body, in_specs=[held, whole, held, held, whole, held], out...  16.3 us
    all_to_all x1, blocking collectives, local(): h_in = lax.all_to_all(incoming, AXES, 0, 0, tiled=True)  13.9 us
    all_to_all x1, waiting for transfers between devices, local(): got = lax.all_to_all(message, AXES, 0, 0, tiled=True)  12 us
    all_to_all x1, starting transfers between devices, local(): got = lax.all_to_all(message, AXES, 0, 0, tiled=True)  9.63 us
    pallas_call x1, Pallas kernels, combine(): pl.pallas_call(body, in_specs=[pl.BlockSpec(memory_space=pltpu.SMEM), who...  2.56 us
    ppermute x1, starting transfers between devices, local(): lax.ppermute(x_in[rows - (taps - 1):], AXES, [(p, p + 1) for p in range(p...  2.4 us
  transfers between devices with their start and end apart: 2, of which 2 were waited for; matrix products, arithmetic and copies ran while one was open for 0% of the time, Pallas kernels for 0%

profile of v2, /device:TPU:0, one launch (start us, length us, event | category | flops | bytes accessed | tf_op | source)
XLA Modules:
  0.0 90.3 jit_solution(13431729176212821888)
XLA Ops:
  0.0 0.9 %slice.3 = bf16[3,8192]{1,0:T(4,128)(2,1)S(1)} slice(bf16[128,8192]{1,0:T(8,128)(2,1)} %x_hbm.1), slice={[125:128], [0:8192]} | slice | bytes 98304 | tf_op jit(solution)/shard_map/slice | solution.py:460
  0.9 2.4 %collective-permute-start = (bf16[3,8192]{1,0:T(4,128)(2,1)S(1)}, bf16[3,8192]{1,0:T(4,128)(2,1)S(1)}, u32[]{:S(2)}, u32[]{:S(2)}) collective-permute-start(bf16[3,8192]{1,0:T(4,128)(2,1)S(1)} %slice.3), channel_id=1, source_target_pairs={{0,1},{1,2},{2,3},{3,4},{4,5},{5,6},{6,7},{7,8},{8,9},{9,10},{10,1... | collective-permute-start | bytes 147464 | tf_op jit(solution)/shard_map/ppermute | solution.py:460
  3.4 0.9 collective-permute-done.halo_hbm
  4.2 0.0 copy-start.1
  4.2 0.6 copy-done.1
  4.9 30.3 %front.1 = (f32[128,8192]{1,0:T(8,128)}, bf16[128,8192]{1,0:T(8,128)(2,1)}, bf16[32,40,128]{2,1,0:T(8,128)(2,1)}, f32[128,32]{1,0:T(8,128)}) custom-call(bf16[128,8192]{1,0:T(8,128)(2,1)} %x_hbm.1, bf16[3,8192]{1,0:T(4,128)(2,1)} %copy-done.1, f32[4,8192]{1,0:T(4,128)} %cw_hbm.1, f32[1,8192]{1,0:T(1,128)} %bitcast.6, bf16[288,8192]{1,0:T(8,128)(2,1)} %bitcast.5, ...), custom_call_target="tpu_custom_call" | custom-call | tf_op jit(solution)/shard_map/front/pallas_call | solution.py:274
  35.1 9.6 %all-to-all-start = ((bf16[32,40,128]{2,1,0:T(8,128)(2,1)}), bf16[32,40,128]{2,1,0:T(8,128)(2,1)S(1)}, u32[]{:S(2)}, u32[]{:S(2)}) async-start(bf16[32,40,128]{2,1,0:T(8,128)(2,1)} %get-tuple-element.10), calls=%async_computation | async-start | bytes 655360 | tf_op jit(solution)/shard_map/all_to_all | solution.py:465
  44.8 12.0 %all-to-all-done.msg_ref = bf16[32,40,128]{2,1,0:T(8,128)(2,1)S(1)} async-done(((bf16[32,40,128]{2,1,0:T(8,128)(2,1)}), bf16[32,40,128]{2,1,0:T(8,128)(2,1)S(1)}, u32[]{:S(2)}, u32[]{:S(2)}) %all-to-all-start) | async-done | bytes 327712 | tf_op jit(solution)/shard_map/all_to_all | solution.py:465
  56.8 0.0 copy-start
  56.8 0.7 copy-done
  57.5 2.6 %combine.1 = bf16[32,32,128]{2,1,0:T(8,128)(2,1)} custom-call(s32[1]{0:T(128)} %bitcast.4.mine_ref, bf16[32,40,128]{2,1,0:T(8,128)(2,1)} %copy-done, f32[16,8192]{1,0:T(8,128)} %a_hbm.5), custom_call_target="tpu_custom_call" | custom-call | tf_op jit(solution)/shard_map/combine/pallas_call | solution.py:349
  60.1 13.9 %all_to_all.10.h_ref = bf16[32,32,128]{2,1,0:T(8,128)(2,1)} all-to-all(bf16[32,32,128]{2,1,0:T(8,128)(2,1)} %combine.1), channel_id=1, replica_groups=mesh['outer'=8,'inner'=4] {'outer','inner'}, dimensions={0} | all-to-all | bytes 524288 | tf_op jit(solution)/shard_map/all_to_all | solution.py:467
  74.0 16.3 %final.1 = bf16[128,8192]{1,0:T(8,128)(2,1)} custom-call(bf16[128,8192]{1,0:T(8,128)(2,1)} %get-tuple-element.9.cum_hbm, bf16[32,32,128]{2,1,0:T(8,128)(2,1)} %all_to_all.10.h_ref, f32[128,8192]{1,0:T(8,128)} %get-tuple-element.11.y_hbm, bf16[128,8192]{1,0:T(8,128)(2,1)} %gate_hbm.1, f32[128,32]{1,0:T(8,128)} %get-tuple-element.12.bc_ref, f32[16,8192]{1,0:T(8,128)} %a_hbm.5), custom_call_target="tpu_custom_call" | custom-call | tf_op jit(solution)/shard_map/final/pallas_call | solution.py:434
Async XLA Ops:
  0.9 3.3 %collective-permute-start = (bf16[3,8192]{1,0:T(4,128)(2,1)S(1)}, bf16[3,8192]{1,0:T(4,128)(2,1)S(1)}, u32[]{:S(2)}, u32[]{:S(2)}) collective-permute-start(bf16[3,8192]{1,0:T(4,128)(2,1)S(1)} %slice.3), channel_id=1, source_target_pairs={{0,1},{1,2},{2,3},{3,4},{4,5},{5,6},{6,7},{7,8},{8,9},{9,10},{10,1... | collective-permute-start | bytes 147464 | tf_op jit(solution)/shard_map/ppermute | solution.py:460
  4.2 0.6 copy-start.1
  35.1 21.7 %all-to-all-start = ((bf16[32,40,128]{2,1,0:T(8,128)(2,1)}), bf16[32,40,128]{2,1,0:T(8,128)(2,1)S(1)}, u32[]{:S(2)}, u32[]{:S(2)}) async-start(bf16[32,40,128]{2,1,0:T(8,128)(2,1)} %get-tuple-element.10), calls=%async_computation | async-start | bytes 655360 | tf_op jit(solution)/shard_map/all_to_all | solution.py:465
  56.8 0.7 copy-start

commit v3 on v2

--- a/solution.py
+++ b/solution.py
@@ -352,6 +352,7 @@
         out_specs=whole,
         out_shape=jax.ShapeDtypeStruct((parts, share.rows, share.lanes), BF16),
         scratch_shapes=[pltpu.VMEM((states, share.width), F32), pltpu.SemaphoreType.DMA((1,))],
+        compiler_params=pltpu.CompilerParams(vmem_limit_bytes=8 * 2**20),
         name="combine",
     )(mine[None], message, decay)
 

time: 90.7 us -> 86.6 us (0.955)
  Pallas kernels: 49.1 us -> 46.8 us
    pallas_call x1, Pallas kernels: 2.56 us -> 0.17 us  [combine(): pl.pallas_call(body, in_specs=[pl.BlockSpec(memory_space=pltpu.SMEM), who...]
    all_to_all x1, blocking collectives: 13.9 us -> 13 us  [local(): h_in = lax.all_to_all(incoming, AXES, 0, 0, tiled=True)]
where the time goes in v3:
time: 86.6 us; the launch traced here: 86.3 us
  Pallas kernels  46.8 us (54%)
  blocking collectives  13 us (15%)
  waiting for transfers between devices  12.9 us (15%)
  starting transfers between devices  12 us (14%)
  local copies, waits for them, and re-layouts  1.57 us (2%)
    pallas_call x1, Pallas kernels, front(): pl.pallas_call(body, in_specs=[held] * 9, out_specs=[held, held, whole, w...  30.3 us
    pallas_call x1, Pallas kernels, final(): pl.pallas_call(body, in_specs=[held, whole, held, held, whole, held], out...  16.3 us
    all_to_all x1, blocking collectives, local(): h_in = lax.all_to_all(incoming, AXES, 0, 0, tiled=True)  13 us
    all_to_all x1, waiting for transfers between devices, local(): got = lax.all_to_all(message, AXES, 0, 0, tiled=True)  12 us
    all_to_all x1, starting transfers between devices, local(): got = lax.all_to_all(message, AXES, 0, 0, tiled=True)  9.63 us
    ppermute x1, starting transfers between devices, local(): lax.ppermute(x_in[rows - (taps - 1):], AXES, [(p, p + 1) for p in range(p...  2.4 us
  transfers between devices with their start and end apart: 2, of which 2 were waited for; matrix products, arithmetic and copies ran while one was open for 0% of the time, Pallas kernels for 0%

profile of v3, /device:TPU:0, one launch (start us, length us, event | category | flops | bytes accessed | tf_op | source)
XLA Modules:
  0.0 86.3 jit_solution(1071659198005764473)
XLA Ops:
  0.0 0.9 %slice.3 = bf16[3,8192]{1,0:T(4,128)(2,1)S(1)} slice(bf16[128,8192]{1,0:T(8,128)(2,1)} %x_hbm.1), slice={[125:128], [0:8192]} | slice | bytes 98304 | tf_op jit(solution)/shard_map/slice | solution.py:461
  0.9 2.4 %collective-permute-start = (bf16[3,8192]{1,0:T(4,128)(2,1)S(1)}, bf16[3,8192]{1,0:T(4,128)(2,1)S(1)}, u32[]{:S(2)}, u32[]{:S(2)}) collective-permute-start(bf16[3,8192]{1,0:T(4,128)(2,1)S(1)} %slice.3), channel_id=1, source_target_pairs={{0,1},{1,2},{2,3},{3,4},{4,5},{5,6},{6,7},{7,8},{8,9},{9,10},{10,1... | collective-permute-start | bytes 147464 | tf_op jit(solution)/shard_map/ppermute | solution.py:461
  3.4 0.9 %collective-permute-done.halo_hbm = bf16[3,8192]{1,0:T(4,128)(2,1)S(1)} collective-permute-done((bf16[3,8192]{1,0:T(4,128)(2,1)S(1)}, bf16[3,8192]{1,0:T(4,128)(2,1)S(1)}, u32[]{:S(2)}, u32[]{:S(2)}) %collective-permute-start) | collective-permute-done | bytes 49184 | tf_op jit(solution)/shard_map/ppermute | solution.py:461
  4.2 0.0 copy-start.1
  4.2 0.6 copy-done.1
  4.9 0.0 copy-start
  4.9 30.3 %front.1 = (f32[128,8192]{1,0:T(8,128)}, bf16[128,8192]{1,0:T(8,128)(2,1)}, bf16[32,40,128]{2,1,0:T(8,128)(2,1)}, f32[128,32]{1,0:T(8,128)}) custom-call(bf16[128,8192]{1,0:T(8,128)(2,1)} %x_hbm.1, bf16[3,8192]{1,0:T(4,128)(2,1)} %copy-done.1, f32[4,8192]{1,0:T(4,128)} %cw_hbm.1, f32[1,8192]{1,0:T(1,128)} %bitcast.6, bf16[288,8192]{1,0:T(8,128)(2,1)} %bitcast.5, ...), custom_call_target="tpu_custom_call" | custom-call | tf_op jit(solution)/shard_map/front/pallas_call | solution.py:274
  35.2 9.6 %all-to-all-start = ((bf16[32,40,128]{2,1,0:T(8,128)(2,1)}), bf16[32,40,128]{2,1,0:T(8,128)(2,1)S(1)}, u32[]{:S(2)}, u32[]{:S(2)}) async-start(bf16[32,40,128]{2,1,0:T(8,128)(2,1)} %get-tuple-element.10), calls=%async_computation | async-start | bytes 655360 | tf_op jit(solution)/shard_map/all_to_all | solution.py:466
  44.8 12.0 %all-to-all-done.msg_ref = bf16[32,40,128]{2,1,0:T(8,128)(2,1)S(1)} async-done(((bf16[32,40,128]{2,1,0:T(8,128)(2,1)}), bf16[32,40,128]{2,1,0:T(8,128)(2,1)S(1)}, u32[]{:S(2)}, u32[]{:S(2)}) %all-to-all-start) | async-done | bytes 327712 | tf_op jit(solution)/shard_map/all_to_all | solution.py:466
  56.9 0.0 copy-done
  56.9 0.2 combine.1
  57.0 13.0 %all_to_all.10.h_ref = bf16[32,32,128]{2,1,0:T(8,128)(2,1)} all-to-all(bf16[32,32,128]{2,1,0:T(8,128)(2,1)S(1)} %combine.1), channel_id=1, replica_groups=mesh['outer'=8,'inner'=4] {'outer','inner'}, dimensions={0} | all-to-all | bytes 524288 | tf_op jit(solution)/shard_map/all_to_all | solution.py:468
  70.0 16.3 %final.1 = bf16[128,8192]{1,0:T(8,128)(2,1)} custom-call(bf16[128,8192]{1,0:T(8,128)(2,1)} %get-tuple-element.9.cum_hbm, bf16[32,32,128]{2,1,0:T(8,128)(2,1)} %all_to_all.10.h_ref, f32[128,8192]{1,0:T(8,128)} %get-tuple-element.11.y_hbm, bf16[128,8192]{1,0:T(8,128)(2,1)} %gate_hbm.1, f32[128,32]{1,0:T(8,128)} %get-tuple-element.12.bc_ref, f32[16,8192]{1,0:T(8,128)} %a_hbm.5), custom_call_target="tpu_custom_call" | custom-call | tf_op jit(solution)/shard_map/final/pallas_call | solution.py:435
Async XLA Ops:
  0.9 3.3 %collective-permute-start = (bf16[3,8192]{1,0:T(4,128)(2,1)S(1)}, bf16[3,8192]{1,0:T(4,128)(2,1)S(1)}, u32[]{:S(2)}, u32[]{:S(2)}) collective-permute-start(bf16[3,8192]{1,0:T(4,128)(2,1)S(1)} %slice.3), channel_id=1, source_target_pairs={{0,1},{1,2},{2,3},{3,4},{4,5},{5,6},{6,7},{7,8},{8,9},{9,10},{10,1... | collective-permute-start | bytes 147464 | tf_op jit(solution)/shard_map/ppermute | solution.py:461
  4.2 0.6 copy-start.1
  4.9 52.0 %copy-start = (f32[16,8192]{1,0:T(8,128)S(1)}, f32[16,8192]{1,0:T(8,128)}, u32[]{:S(2)}) copy-start(f32[16,8192]{1,0:T(8,128)} %a_hbm.5) | copy-start | bytes 1572868
  35.2 21.7 %all-to-all-start = ((bf16[32,40,128]{2,1,0:T(8,128)(2,1)}), bf16[32,40,128]{2,1,0:T(8,128)(2,1)S(1)}, u32[]{:S(2)}, u32[]{:S(2)}) async-start(bf16[32,40,128]{2,1,0:T(8,128)(2,1)} %get-tuple-element.10), calls=%async_computation | async-start | bytes 655360 | tf_op jit(solution)/shard_map/all_to_all | solution.py:466

commit v4 on v3

--- a/solution.py
+++ b/solution.py
@@ -65,11 +65,11 @@
     rank = dt_proj.shape[0]
     states = decay.shape[0]
     columns = x_proj_t.shape[0]
-    block = pick_block(width, 1024)
+    block = pick_block(width, 2048)
     count = width // block
     per_block = block // share.width
     groups = rows // GROUP
-    wide = pick_block(width, 1024)
+    wide = pick_block(width, 2048)
     chunks = width // wide
     ratio = wide // block
 
@@ -360,8 +360,8 @@
 def final(cum, h_in, y, gate, bc, decay, share):
     rows, width = cum.shape
     states = decay.shape[0]
-    wide = pick_block(width, 1024)
-    block = pick_block(wide, 256)
+    wide = pick_block(width, 2048)
+    block = wide
     count = width // block
     chunks = width // wide
     ratio = wide // block

time: 86.6 us -> 81.6 us (0.942)
  Pallas kernels: 46.8 us -> 41.8 us
    pallas_call x1, Pallas kernels: 16.3 us -> 13.4 us  [final(): pl.pallas_call(body, in_specs=[held, whole, held, held, whole, held], out...]
    pallas_call x1, Pallas kernels: 30.3 us -> 28.2 us  [front(): pl.pallas_call(body, in_specs=[held] * 9, out_specs=[held, held, whole, w...]
where the time goes in v4:
time: 81.6 us; the launch traced here: 81.3 us
  Pallas kernels  41.8 us (51%)
  blocking collectives  13 us (16%)
  waiting for transfers between devices  12.9 us (16%)
  starting transfers between devices  12 us (15%)
  local copies, waits for them, and re-layouts  1.57 us (2%)
    pallas_call x1, Pallas kernels, front(): pl.pallas_call(body, in_specs=[held] * 9, out_specs=[held, held, whole, w...  28.2 us
    pallas_call x1, Pallas kernels, final(): pl.pallas_call(body, in_specs=[held, whole, held, held, whole, held], out...  13.4 us
    all_to_all x1, blocking collectives, local(): h_in = lax.all_to_all(incoming, AXES, 0, 0, tiled=True)  13 us
    all_to_all x1, waiting for transfers between devices, local(): got = lax.all_to_all(message, AXES, 0, 0, tiled=True)  12 us
    all_to_all x1, starting transfers between devices, local(): got = lax.all_to_all(message, AXES, 0, 0, tiled=True)  9.62 us
    ppermute x1, starting transfers between devices, local(): lax.ppermute(x_in[rows - (taps - 1):], AXES, [(p, p + 1) for p in range(p...  2.4 us
  transfers between devices with their start and end apart: 2, of which 2 were waited for; matrix products, arithmetic and copies ran while one was open for 0% of the time, Pallas kernels for 0%

profile of v4, /device:TPU:0, one launch (start us, length us, event | category | flops | bytes accessed | tf_op | source)
XLA Modules:
  0.0 81.3 jit_solution(15454271835041804878)
XLA Ops:
  0.0 0.9 %slice.3 = bf16[3,8192]{1,0:T(4,128)(2,1)S(1)} slice(bf16[128,8192]{1,0:T(8,128)(2,1)} %x_hbm.1), slice={[125:128], [0:8192]} | slice | bytes 98304 | tf_op jit(solution)/shard_map/slice | solution.py:461
  0.9 2.4 %collective-permute-start = (bf16[3,8192]{1,0:T(4,128)(2,1)S(1)}, bf16[3,8192]{1,0:T(4,128)(2,1)S(1)}, u32[]{:S(2)}, u32[]{:S(2)}) collective-permute-start(bf16[3,8192]{1,0:T(4,128)(2,1)S(1)} %slice.3), channel_id=1, source_target_pairs={{0,1},{1,2},{2,3},{3,4},{4,5},{5,6},{6,7},{7,8},{8,9},{9,10},{10,1... | collective-permute-start | bytes 147464 | tf_op jit(solution)/shard_map/ppermute | solution.py:461
  3.4 0.9 %collective-permute-done.halo_hbm = bf16[3,8192]{1,0:T(4,128)(2,1)S(1)} collective-permute-done((bf16[3,8192]{1,0:T(4,128)(2,1)S(1)}, bf16[3,8192]{1,0:T(4,128)(2,1)S(1)}, u32[]{:S(2)}, u32[]{:S(2)}) %collective-permute-start) | collective-permute-done | bytes 49184 | tf_op jit(solution)/shard_map/ppermute | solution.py:461
  4.2 0.0 copy-start.1
  4.2 0.6 copy-done.1
  4.9 0.0 copy-start
  4.9 28.2 %front.1 = (f32[128,8192]{1,0:T(8,128)}, bf16[128,8192]{1,0:T(8,128)(2,1)}, bf16[32,40,128]{2,1,0:T(8,128)(2,1)}, f32[128,32]{1,0:T(8,128)}) custom-call(bf16[128,8192]{1,0:T(8,128)(2,1)} %x_hbm.1, bf16[3,8192]{1,0:T(4,128)(2,1)} %copy-done.1, f32[4,8192]{1,0:T(4,128)} %cw_hbm.1, f32[1,8192]{1,0:T(1,128)} %bitcast.6, bf16[288,8192]{1,0:T(8,128)(2,1)} %bitcast.5, ...), custom_call_target="tpu_custom_call" | custom-call | tf_op jit(solution)/shard_map/front/pallas_call | solution.py:274
  33.1 9.6 %all-to-all-start = ((bf16[32,40,128]{2,1,0:T(8,128)(2,1)}), bf16[32,40,128]{2,1,0:T(8,128)(2,1)S(1)}, u32[]{:S(2)}, u32[]{:S(2)}) async-start(bf16[32,40,128]{2,1,0:T(8,128)(2,1)} %get-tuple-element.10), calls=%async_computation | async-start | bytes 655360 | tf_op jit(solution)/shard_map/all_to_all | solution.py:466
  42.7 12.0 %all-to-all-done.msg_ref = bf16[32,40,128]{2,1,0:T(8,128)(2,1)S(1)} async-done(((bf16[32,40,128]{2,1,0:T(8,128)(2,1)}), bf16[32,40,128]{2,1,0:T(8,128)(2,1)S(1)}, u32[]{:S(2)}, u32[]{:S(2)}) %all-to-all-start) | async-done | bytes 327712 | tf_op jit(solution)/shard_map/all_to_all | solution.py:466
  54.8 0.0 copy-done
  54.8 0.2 combine.1
  55.0 13.0 %all_to_all.10.h_ref = bf16[32,32,128]{2,1,0:T(8,128)(2,1)} all-to-all(bf16[32,32,128]{2,1,0:T(8,128)(2,1)S(1)} %combine.1), channel_id=1, replica_groups=mesh['outer'=8,'inner'=4] {'outer','inner'}, dimensions={0} | all-to-all | bytes 524288 | tf_op jit(solution)/shard_map/all_to_all | solution.py:468
  67.9 13.4 %final.1 = bf16[128,8192]{1,0:T(8,128)(2,1)} custom-call(bf16[128,8192]{1,0:T(8,128)(2,1)} %get-tuple-element.9.cum_hbm, bf16[32,32,128]{2,1,0:T(8,128)(2,1)} %all_to_all.10.h_ref, f32[128,8192]{1,0:T(8,128)} %get-tuple-element.11.y_hbm, bf16[128,8192]{1,0:T(8,128)(2,1)} %gate_hbm.1, f32[128,32]{1,0:T(8,128)} %get-tuple-element.12.bc_ref, f32[16,8192]{1,0:T(8,128)} %a_hbm.5), custom_call_target="tpu_custom_call" | custom-call | tf_op jit(solution)/shard_map/final/pallas_call | solution.py:435
Async XLA Ops:
  0.9 3.3 %collective-permute-start = (bf16[3,8192]{1,0:T(4,128)(2,1)S(1)}, bf16[3,8192]{1,0:T(4,128)(2,1)S(1)}, u32[]{:S(2)}, u32[]{:S(2)}) collective-permute-start(bf16[3,8192]{1,0:T(4,128)(2,1)S(1)} %slice.3), channel_id=1, source_target_pairs={{0,1},{1,2},{2,3},{3,4},{4,5},{5,6},{6,7},{7,8},{8,9},{9,10},{10,1... | collective-permute-start | bytes 147464 | tf_op jit(solution)/shard_map/ppermute | solution.py:461
  4.2 0.6 copy-start.1
  4.9 49.9 %copy-start = (f32[16,8192]{1,0:T(8,128)S(1)}, f32[16,8192]{1,0:T(8,128)}, u32[]{:S(2)}) copy-start(f32[16,8192]{1,0:T(8,128)} %a_hbm.5) | copy-start | bytes 1572868
  33.1 21.7 %all-to-all-start = ((bf16[32,40,128]{2,1,0:T(8,128)(2,1)}), bf16[32,40,128]{2,1,0:T(8,128)(2,1)S(1)}, u32[]{:S(2)}, u32[]{:S(2)}) async-start(bf16[32,40,128]{2,1,0:T(8,128)(2,1)} %get-tuple-element.10), calls=%async_computation | async-start | bytes 655360 | tf_op jit(solution)/shard_map/all_to_all | solution.py:466
